TPU v7x, 32 devices: a whole 2x2x4 slice. The times are simulated.
32 devices in a mesh: parts: 2 (over x), sub: 16 (over z, y, core).
Axes of the slice: x: 2, y: 2, z: 4, core: 2. Of those that a mesh axis runs over, the one named last changes fastest.
Arguments:
- right_side: float32 [32768, 256], P(('parts', 'sub')), parts along dimension 0, may hold values from -6 to 6
- face_weight: float32 [64, 512], P(('parts', 'sub')), parts along dimension 0, may hold values from 0.2 to 0.8
- schur: bfloat16 [65536, 1024], P(('parts', 'sub')), parts along dimension 0, as said below
- neumann: bfloat16 [65536, 1024], P(('parts', 'sub')), parts along dimension 0
- constraint: bfloat16 [2048, 512], P(('parts', 'sub')), parts along dimension 0, may hold values from -0.25 to 0.25
- coarse_inverse: bfloat16 [2048, 1024], P(('parts', 'sub')), parts along dimension 0
Outputs:
- solution: float32 [32768, 256], P(('parts', 'sub')), parts along dimension 0
- residual: float32 [32768, 256], P(('parts', 'sub')), parts along dimension 0
There are 2 independent parts, one for each index of `parts`. A program takes and returns all parts, laid end to end along the dimension named above; each array names one. Nothing has to cross between parts.
Inputs may be any that keep to these rules, and one draw needn't show every extreme that they name: schur, neumann and coarse_inverse are symmetric, and each block schur_j, neumann_j and the whole coarse_inverse is positive definite.
All inputs are finite; a program needn't handle non-finite values.
Results may differ from a plain program's by a relative error of at most 0.0091.
Values may be sent and summed in bfloat16 or wider, within the bound.
A program may use at most 64 MiB of HBM per device.

v0:
```python
import functools

import jax
import jax.numpy as jnp
from jax import lax
from jax.experimental import pallas as pl
from jax.experimental.pallas import tpu as pltpu
from jax.sharding import PartitionSpec as P

MESH = pl.DeviceIdType.MESH
STREAMS = 2
VMEM = 67043328
F32, BF16 = jnp.float32, jnp.bfloat16

INIT_P, N0_P, N0_Q, S0_P, S0_Q, N1_P, N1_Q, S1_Q = range(8)
MESSAGES = 8


def dot(a, b):
    return jnp.dot(a, b, preferred_element_type=F32)


def dot_first(a, b):
    return lax.dot_general(a, b, (((0,), (0,)), ((), ())), preferred_element_type=F32)


def column_sum(value):
    return jnp.sum(value, axis=0, keepdims=True)


def kernel(
    n, streams,
    rs_hbm, w_hbm, schur_hbm, neumann_hbm, con_hbm, ainv_hbm,
    sol_ref, out_ref,
    rs, w, w_left, schur, neumann, con, ainv, wb,
    res, part, dirn, image, zed,
    sent, came, coarse0, coarse1, slots1, slots2,
    load_sem, aux_sem, msg_send, msg_recv, ag_sem, ar_sem,
):
    ls, nf = w_hbm.shape
    ni = schur_hbm.shape[1]
    ncf = con_hbm.shape[0] // ls
    cw = rs_hbm.shape[1] // streams
    me = lax.axis_index("sub")
    right, left = lax.rem(me + 1, n), lax.rem(me + n - 1, n)
    core, chip = lax.rem(me, 2), me // 2
    partner = chip * 2 + 1 - core

    loads = [
        pltpu.make_async_copy(src, dst, load_sem.at[i])
        for i, (src, dst) in enumerate((
            (rs_hbm, rs), (w_hbm, w),
            (con_hbm, con.at[pl.ds(ncf, ls * ncf)]),
            (ainv_hbm, ainv.at[pl.ds(ncf, ls * ncf)]),
            (neumann_hbm, neumann), (schur_hbm, schur),
        ))
    ]
    for load in loads:
        load.start()

    barrier = pltpu.get_barrier_semaphore()

    def greet(k, carry):
        pl.semaphore_signal(barrier, inc=1, device_id={"sub": lax.rem(me + k, n)}, device_id_type=MESH)
        return carry

    lax.fori_loop(1, n, greet, 0)

    blocks = (coarse0, coarse1)

    def columns(st):
        return pl.ds(st * cw, cw)

    def face(f):
        return pl.ds(f * nf, nf)

    def message(st, m):
        to_right = m in (INIT_P, N0_P, S0_P, N1_P)
        return pltpu.make_async_remote_copy(
            src_ref=sent.at[st, m], dst_ref=came.at[st, m],
            send_sem=msg_send.at[st, m], recv_sem=msg_recv.at[st, m],
            device_id={"sub": right if to_right else left}, device_id_type=MESH,
        )

    def send(st, m, value):
        sent[st, m] = value.astype(BF16)
        message(st, m).start()

    def receive(st, m):
        message(st, m).wait_recv()
        return came[st, m].astype(F32)

    def gather_copy(inst, st, target):
        block = blocks[inst].at[st, chip, core]
        return pltpu.make_async_remote_copy(
            src_ref=block, dst_ref=block, send_sem=ag_sem.at[inst, st, 0], recv_sem=ag_sem.at[inst, st, 1],
            device_id={"sub": target}, device_id_type=MESH,
        )

    def gather_all(inst, st):
        most = blocks[inst].at[st, pl.ds(0, n // 2 - 1), core]
        return pltpu.make_async_remote_copy(
            src_ref=most, dst_ref=most, send_sem=ag_sem.at[inst, st, 0], recv_sem=ag_sem.at[inst, st, 1],
            device_id={"sub": partner}, device_id_type=MESH,
        )

    def gather_relay(inst, st, side):
        half = blocks[inst].at[st, :, side]
        return pltpu.make_async_remote_copy(
            src_ref=half, dst_ref=half, send_sem=ag_sem.at[inst, st, 2], recv_sem=ag_sem.at[inst, st, 3],
            device_id={"sub": partner}, device_id_type=MESH,
        )

    def restrict(st, vector, faces):
        return jnp.concatenate(
            [dot(con[pl.ds(f * ncf, ncf), :], vector[face(f), columns(st)].astype(BF16)) for f in faces], axis=0
        )

    def coarse_start(inst, st, value):
        blocks[inst][st, chip, core] = value.astype(BF16)

    def coarse_send(inst, st):
        def one(k, carry):
            gather_copy(inst, st, lax.rem(me + 2 * k, n)).start()
            return carry

        lax.fori_loop(1, n // 2, one, 0)

    def coarse_relay(inst, st):
        gather_all(inst, st).wait_recv()
        gather_relay(inst, st, core).start()

    def coarse_finish(inst, st):
        gather_relay(inst, st, 1 - core).wait_recv()
        gathered = blocks[inst][st].reshape(n, -1, cw)
        if inst == 1:
            shares = gathered.astype(F32)
            shared = jnp.concatenate([shares[1:, :ncf], shares[:1, :ncf]], axis=0) + shares[:, ls * ncf :]
            gathered = jnp.concatenate([shares[:, ncf : ls * ncf], shared], axis=1).astype(BF16)
        return dot(ainv[...], gathered.reshape(-1, cw))

    def reduce_copy(slots, inst, st, target):
        return pltpu.make_async_remote_copy(
            src_ref=slots.at[st, me], dst_ref=slots.at[st, me],
            send_sem=ar_sem.at[inst, st, 0], recv_sem=ar_sem.at[inst, st, 1],
            device_id={"sub": target}, device_id_type=MESH,
        )

    def reduce_most(slots, inst, st):
        most = slots.at[st, pl.ds(0, n - 1)]
        return pltpu.make_async_remote_copy(
            src_ref=most, dst_ref=most, send_sem=ar_sem.at[inst, st, 0], recv_sem=ar_sem.at[inst, st, 1],
            device_id={"sub": partner}, device_id_type=MESH,
        )

    def reduce_start(slots, inst, st, rows):
        slots[st, me] = jnp.concatenate(rows, axis=0)

        def one(k, carry):
            reduce_copy(slots, inst, st, lax.rem(me + k, n)).start()
            return carry

        lax.fori_loop(1, n, one, 0)

    def reduce_finish(slots, inst, st):
        reduce_most(slots, inst, st).wait_recv()
        return jnp.sum(slots[st], axis=0)

    def apply(st, kind, vector, order, before, p_message, q_message):
        cs = columns(st)
        matrix = neumann if kind == "n" else schur
        seen = []
        for s in order:
            before(s)
            lower, upper = vector[face(s), cs], vector[face(s + 1), cs]
            if kind == "n":
                lower, upper = (1.0 - wb[s]) * lower, wb[s + 1] * upper
            stacked = jnp.concatenate([lower.astype(BF16), upper.astype(BF16)], axis=0)
            halves = (0, 1) if s == 0 else (1, 0)
            for half in halves:
                f = s + half
                product = dot(matrix[pl.ds(s * ni + half * nf, nf), :], stacked)
                if kind == "n":
                    product = product * (wb[f] if half == 1 else 1.0 - wb[f])
                if f in seen:
                    part[face(f), cs] = part[face(f), cs] + product
                else:
                    part[face(f), cs] = product
                seen.append(f)
                if f == 0 and q_message is not None:
                    send(st, q_message, product)
                if f == ls and p_message is not None:
                    send(st, p_message, product)

    def inner(st, first, second, faces):
        total = None
        for f in faces:
            term = column_sum(first[face(f), columns(st)] * second[face(f), columns(st)])
            total = term if total is None else total + term
        return total

    every, owned = range(ls + 1), range(1, ls + 1)
    upward, downward = list(range(ls)), list(range(ls - 1, -1, -1))
    sts = range(streams)

    loads[0].wait()
    loads[2].wait()
    x0, alpha0 = {}, {}
    for st in sts:
        cs = columns(st)
        sent[st, INIT_P] = rs[face(ls - 1), cs].astype(BF16)
        for f in range(ls):
            res[face(f + 1), cs] = rs[face(f), cs]
    loads[1].wait()
    c32 = {st: restrict(st, res, owned) for st in sts}
    for st in sts:
        coarse_start(0, st, c32[st])
    pl.semaphore_wait(barrier, n - 1)

    last_rows = pl.ds((ls - 1) * ncf, ncf)
    aux = [
        pltpu.make_async_remote_copy(
            src_ref=src, dst_ref=dst, send_sem=aux_sem.at[i, 0], recv_sem=aux_sem.at[i, 1],
            device_id={"sub": right}, device_id_type=MESH,
        )
        for i, (src, dst) in enumerate((
            (w_hbm, w_left),
            (ainv_hbm.at[last_rows], ainv.at[pl.ds(0, ncf)]),
            (con_hbm.at[last_rows], con.at[pl.ds(0, ncf)]),
        ))
    ]
    aux[0].start()
    for st in sts:
        message(st, INIT_P).start()
    for st in sts:
        coarse_send(0, st)
    aux[1].start()
    aux[2].start()

    def spread(row):
        return jnp.transpose(jnp.broadcast_to(row, (cw, nf)))

    for f in range(ls):
        wb[f + 1] = spread(w[pl.ds(f, 1), :])

    loads[4].wait()

    def precondition(inst, before, order, p_message, q_message):
        coupled = {}
        for st in sts:
            apply(st, "n", res, order, functools.partial(before, st), p_message, q_message)
            coupled[st] = inner(st, res, part, every)
        return coupled

    def assemble(inst, st, target, coupled, p_message, q_message):
        cs = columns(st)
        x32 = coarse_finish(inst, st)
        if inst == 0:
            x0[st] = x32
        else:
            x32 = x0[st] - alpha0[st] * x32
        x = x32.astype(BF16)
        norm = coupled + column_sum(c32[st] * x[ncf:, :].astype(F32))
        for f in every:
            value = part[face(f), cs] + dot_first(con[pl.ds(f * ncf, ncf), :], x[f * ncf : (f + 1) * ncf, :])
            if f == 0:
                value = value + receive(st, p_message)
            if f == ls:
                value = value + receive(st, q_message)
            target[face(f), cs] = value
        return norm

    def first_face(st, s):
        if s != 0:
            return
        if st == 0:
            aux[0].wait_recv()
            wb[0] = spread(w_left[pl.ds(ls - 1, 1), :])
        res[face(0), columns(st)] = receive(st, INIT_P)

    nothing = lambda s: None

    coupled = precondition(0, first_face, downward, N0_P, N0_Q)
    coarse_relay(0, 0)
    loads[3].wait()
    aux[1].wait_recv()
    aux[2].wait_recv()
    loads[5].wait()
    rows0 = {}
    for st in sts:
        norm = assemble(0, st, dirn, coupled[st], N0_P, N0_Q)
        if st + 1 < streams:
            coarse_relay(0, st + 1)
        apply(st, "s", dirn, upward, nothing, S0_P, S0_Q)
        reduce_start(slots1, 0, st, [norm, inner(st, dirn, part, every)])
        coarse_start(1, st, restrict(st, part, every))
        coarse_send(1, st)
    norm0, bent0, coupled = {}, {}, {}
    for st in sts:
        cs = columns(st)
        total = reduce_finish(slots1, 0, st)
        norm0[st], bent0[st] = total[0:1], total[1:2]
        alpha0[st] = norm0[st] / bent0[st]
        for f in every:
            value = part[face(f), cs]
            if f == 0:
                value = value + receive(st, S0_P)
            if f == ls:
                value = value + receive(st, S0_Q)
            image[face(f), cs] = value
            res[face(f), cs] = res[face(f), cs] - alpha0[st] * value
        apply(st, "n", res, downward, nothing, N1_P, N1_Q)
        c32[st] = restrict(st, res, owned)
        coupled[st] = inner(st, res, part, every)
    coarse_relay(1, 0)
    for st in sts:
        norm = assemble(1, st, zed, coupled[st], N1_P, N1_Q)
        if st + 1 < streams:
            coarse_relay(1, st + 1)
        apply(st, "s", zed, upward, nothing, None, S1_Q)
        reduce_start(slots2, 1, st, [
            norm, inner(st, zed, part, every), inner(st, zed, image, owned), jnp.zeros_like(norm),
        ])
    for st in sts:
        cs = columns(st)
        total = reduce_finish(slots2, 1, st)
        norm1 = total[0:1]
        beta = norm1 / norm0[st]
        bent1 = total[1:2] + beta * (2.0 * total[2:3] + beta * bent0[st])
        alpha1 = norm1 / bent1
        for f in owned:
            own = pl.ds((f - 1) * nf, nf)
            direction = zed[face(f), cs] + beta * dirn[face(f), cs]
            sol_ref[own, cs] = alpha0[st] * dirn[face(f), cs] + alpha1 * direction
            value = part[face(f), cs]
            if f == ls:
                value = value + receive(st, S1_Q)
            value = value + beta * image[face(f), cs]
            out_ref[own, cs] = res[face(f), cs] - alpha1 * value

    for copy in aux:
        copy.wait_send()
    for st in sts:
        for m in range(MESSAGES):
            message(st, m).wait_send()
        for inst in range(2):
            gather_all(inst, st).wait_send()
            gather_relay(inst, st, core).wait_send()
        reduce_most(slots1, 0, st).wait_send()
        reduce_most(slots2, 1, st).wait_send()


def deliver(sol_ref, res_ref, sol_hbm, res_hbm, sem):
    copies = [
        pltpu.make_async_copy(sol_ref, sol_hbm, sem.at[0]),
        pltpu.make_async_copy(res_ref, res_hbm, sem.at[1]),
    ]
    for copy in copies:
        copy.start()
    for copy in copies:
        copy.wait()


def solution(mesh):
    n = mesh.shape["sub"]

    def shards(right_side, face_weight, schur, neumann, constraint, coarse_inverse):
        ls, nf = face_weight.shape
        rows, r = right_side.shape
        lc = constraint.shape[0]
        ncf = lc // ls
        streams = STREAMS
        cw = r // streams
        extended = rows + nf
        any_spec = pl.BlockSpec(memory_space=pltpu.HBM)
        vmem_spec = pl.BlockSpec(memory_space=pltpu.VMEM)
        results = pl.pallas_call(
            functools.partial(kernel, n, streams),
            name="interface_cg",
            out_shape=(pltpu.VMEM((rows, r), F32),) * 2,
            in_specs=[any_spec] * 6,
            out_specs=(vmem_spec,) * 2,
            scratch_shapes=[
                pltpu.VMEM((rows, r), F32),
                pltpu.VMEM((ls, nf), F32),
                pltpu.VMEM((ls, nf), F32),
                pltpu.VMEM(schur.shape, BF16),
                pltpu.VMEM(neumann.shape, BF16),
                pltpu.VMEM((lc + ncf, nf), BF16),
                pltpu.VMEM((lc + ncf, coarse_inverse.shape[1]), BF16),
                pltpu.VMEM((ls + 1, nf, cw), F32),
                pltpu.VMEM((extended, r), F32),
                pltpu.VMEM((extended, r), F32),
                pltpu.VMEM((extended, r), F32),
                pltpu.VMEM((extended, r), F32),
                pltpu.VMEM((extended, r), F32),
                pltpu.VMEM((streams, MESSAGES, nf, cw), BF16),
                pltpu.VMEM((streams, MESSAGES, nf, cw), BF16),
                pltpu.VMEM((streams, n // 2, 2, lc, cw), BF16),
                pltpu.VMEM((streams, n // 2, 2, lc + ncf, cw), BF16),
                pltpu.VMEM((streams, n, 2, cw), F32),
                pltpu.VMEM((streams, n, 4, cw), F32),
                pltpu.SemaphoreType.DMA((6,)),
                pltpu.SemaphoreType.DMA((3, 2)),
                pltpu.SemaphoreType.DMA((streams, MESSAGES)),
                pltpu.SemaphoreType.DMA((streams, MESSAGES)),
                pltpu.SemaphoreType.DMA((2, streams, 4)),
                pltpu.SemaphoreType.DMA((2, streams, 2)),
            ],
            compiler_params=pltpu.CompilerParams(
                collective_id=0, has_side_effects=True, vmem_limit_bytes=VMEM - 2 * 4 * rows * r - 65536
            ),
        )(right_side, face_weight, schur, neumann, constraint, coarse_inverse)
        return pl.pallas_call(
            deliver,
            name="deliver",
            out_shape=(jax.ShapeDtypeStruct((rows, r), F32),) * 2,
            in_specs=[vmem_spec] * 2,
            out_specs=(any_spec,) * 2,
            scratch_shapes=[pltpu.SemaphoreType.DMA((2,))],
            compiler_params=pltpu.CompilerParams(vmem_limit_bytes=8 * 1024 * 1024),
        )(*results)

    spec = P(("parts", "sub"), None)
    return jax.shard_map(
        shards, mesh=mesh, in_specs=(spec,) * 6, out_specs=(spec, spec), check_vma=False
    )
```

profile of v0, /device:TPU:0, one launch (start us, length us, event | category | flops | bytes accessed | tf_op | source)
XLA Modules:
  0.0 49.2 jit_solution(10872007106228417017)
XLA Ops:
  0.6 47.3 %interface_cg.1 = (f32[1024,256]{1,0:T(8,128)S(1)}, f32[1024,256]{1,0:T(8,128)S(1)}) custom-call(f32[1024,256]{1,0:T(8,128)} %rs_hbm.1, f32[2,512]{1,0:T(2,128)} %w_hbm.1, bf16[2048,1024]{1,0:T(8,128)(2,1)} %schur_hbm.1, bf16[2048,1024]{1,0:T(8,128)(2,1)} %neumann_hbm.1, bf16[64,512]{1,0:T(8,128)(2,1)} %con_hbm.1, bf16[64,1024]{1,0:T(8,128)(2,1)} %ainv_hbm.1), custom_call_target="tpu_custom_call" | custom-call | tf_op jit(solution)/shard_map/interface_cg/pallas_call | solution.py:377
  47.9 1.3 %deliver.1 = (f32[1024,256]{1,0:T(8,128)}, f32[1024,256]{1,0:T(8,128)}) custom-call(f32[1024,256]{1,0:T(8,128)S(1)} %get-tuple-element.4.sol_ref, f32[1024,256]{1,0:T(8,128)S(1)} %get-tuple-element.5.res_ref), custom_call_target="tpu_custom_call" | custom-call | tf_op jit(solution)/shard_map/deliver/pallas_call | solution.py:414
where the time goes:
time: 49.4 us; the launch traced here: 49.2 us
  Pallas kernels  48.6 us (98%)
  between operations  0.64 us (1%)
    pallas_call x1, Pallas kernels, shards(): pl.pallas_call(functools.partial(kernel, n, streams), name='interface_cg'...  47.3 us
    pallas_call x1, Pallas kernels, shards(): pl.pallas_call(deliver, name='deliver', out_shape=(jax.ShapeDtypeStruct((...  1.33 us

commit v1 on v0

--- a/solution.py
+++ b/solution.py
@@ -32,7 +32,7 @@
     n, streams,
     rs_hbm, w_hbm, schur_hbm, neumann_hbm, con_hbm, ainv_hbm,
     sol_ref, out_ref,
-    rs, w, w_left, schur, neumann, con, ainv, wb,
+    w, w_left, schur, neumann, con, ainv, wb,
     res, part, dirn, image, zed,
     sent, came, coarse0, coarse1, slots1, slots2,
     load_sem, aux_sem, msg_send, msg_recv, ag_sem, ar_sem,
@@ -46,13 +46,19 @@
     core, chip = lax.rem(me, 2), me // 2
     partner = chip * 2 + 1 - core
 
+    rest, last = pl.ds(0, (ls - 1) * nf), pl.ds((ls - 1) * nf, nf)
+    low, high = pl.ds(0, (ls - 1) * ni), pl.ds((ls - 1) * ni, ni)
     loads = [
         pltpu.make_async_copy(src, dst, load_sem.at[i])
         for i, (src, dst) in enumerate((
-            (rs_hbm, rs), (w_hbm, w),
+            (rs_hbm.at[last], res.at[pl.ds(ls * nf, nf)]),
+            (rs_hbm.at[rest], res.at[pl.ds(nf, (ls - 1) * nf)]),
             (con_hbm, con.at[pl.ds(ncf, ls * ncf)]),
+            (w_hbm, w),
+            (neumann_hbm.at[high], neumann.at[high]),
+            (neumann_hbm.at[low], neumann.at[low]),
             (ainv_hbm, ainv.at[pl.ds(ncf, ls * ncf)]),
-            (neumann_hbm, neumann), (schur_hbm, schur),
+            (schur_hbm, schur),
         ))
     ]
     for load in loads:
@@ -132,12 +138,7 @@
 
     def coarse_finish(inst, st):
         gather_relay(inst, st, 1 - core).wait_recv()
-        gathered = blocks[inst][st].reshape(n, -1, cw)
-        if inst == 1:
-            shares = gathered.astype(F32)
-            shared = jnp.concatenate([shares[1:, :ncf], shares[:1, :ncf]], axis=0) + shares[:, ls * ncf :]
-            gathered = jnp.concatenate([shares[:, ncf : ls * ncf], shared], axis=1).astype(BF16)
-        return dot(ainv[...], gathered.reshape(-1, cw))
+        return dot(ainv[...], blocks[inst][st].reshape(-1, cw))
 
     def reduce_copy(slots, inst, st, target):
         return pltpu.make_async_remote_copy(
@@ -166,31 +167,55 @@
         reduce_most(slots, inst, st).wait_recv()
         return jnp.sum(slots[st], axis=0)
 
-    def apply(st, kind, vector, order, before, p_message, q_message):
-        cs = columns(st)
+    def weighted(kind, f, k, value):
+        if kind == "s":
+            return value
+        return value * (wb[f] if k == 1 else 1.0 - wb[f])
+
+    def operand(st, kind, vector, s, ks):
+        parts = [weighted(kind, s + k, k, vector[face(s + k), columns(st)]).astype(BF16) for k in ks]
+        return parts[0] if len(parts) == 1 else jnp.concatenate(parts, axis=0)
+
+    def product(kind, s, h, ks, value):
         matrix = neumann if kind == "n" else schur
-        seen = []
+        block = matrix[pl.ds(s * ni + h * nf, nf), pl.ds(ks[0] * nf, len(ks) * nf)]
+        return dot(block, value)
+
+    def early(st, kind, vector, late, m, before=None):
+        cs = columns(st)
+        order = list(range(ls)) if late == ls else list(range(ls - 1, -1, -1))
+        seen = set()
         for s in order:
-            before(s)
-            lower, upper = vector[face(s), cs], vector[face(s + 1), cs]
-            if kind == "n":
-                lower, upper = (1.0 - wb[s]) * lower, wb[s + 1] * upper
-            stacked = jnp.concatenate([lower.astype(BF16), upper.astype(BF16)], axis=0)
-            halves = (0, 1) if s == 0 else (1, 0)
-            for half in halves:
-                f = s + half
-                product = dot(matrix[pl.ds(s * ni + half * nf, nf), :], stacked)
-                if kind == "n":
-                    product = product * (wb[f] if half == 1 else 1.0 - wb[f])
+            if before is not None:
+                before(s)
+            ks = [k for k in (0, 1) if s + k != late]
+            value = operand(st, kind, vector, s, ks)
+            for h in (0, 1) if late == ls else (1, 0):
+                f = s + h
+                term = product(kind, s, h, ks, value)
+                if f != late:
+                    term = weighted(kind, f, h, term)
                 if f in seen:
-                    part[face(f), cs] = part[face(f), cs] + product
-                else:
-                    part[face(f), cs] = product
-                seen.append(f)
-                if f == 0 and q_message is not None:
-                    send(st, q_message, product)
-                if f == ls and p_message is not None:
-                    send(st, p_message, product)
+                    term = part[face(f), cs] + term
+                part[face(f), cs] = term
+                seen.add(f)
+                if m is not None and f == ls - late:
+                    send(st, m, term)
+
+    def late_face(st, kind, vector, late, m):
+        cs = columns(st)
+        s, k = (0, 0) if late == 0 else (ls - 1, 1)
+        value = operand(st, kind, vector, s, [k])
+        for h in (k, 1 - k):
+            f = s + h
+            term = product(kind, s, h, [k], value)
+            if f == late:
+                term = weighted(kind, f, h, part[face(f), cs] + term)
+            else:
+                term = part[face(f), cs] + weighted(kind, f, h, term)
+            part[face(f), cs] = term
+            if m is not None and f == late:
+                send(st, m, term)
 
     def inner(st, first, second, faces):
         total = None
@@ -200,18 +225,13 @@
         return total
 
     every, owned = range(ls + 1), range(1, ls + 1)
-    upward, downward = list(range(ls)), list(range(ls - 1, -1, -1))
     sts = range(streams)
 
     loads[0].wait()
+    for st in sts:
+        sent[st, INIT_P] = res[face(ls), columns(st)].astype(BF16)
+    loads[1].wait()
     loads[2].wait()
-    x0, alpha0 = {}, {}
-    for st in sts:
-        cs = columns(st)
-        sent[st, INIT_P] = rs[face(ls - 1), cs].astype(BF16)
-        for f in range(ls):
-            res[face(f + 1), cs] = rs[face(f), cs]
-    loads[1].wait()
     c32 = {st: restrict(st, res, owned) for st in sts}
     for st in sts:
         coarse_start(0, st, c32[st])
@@ -229,9 +249,9 @@
             (con_hbm.at[last_rows], con.at[pl.ds(0, ncf)]),
         ))
     ]
+    for st in sts:
+        message(st, INIT_P).start()
     aux[0].start()
-    for st in sts:
-        message(st, INIT_P).start()
     for st in sts:
         coarse_send(0, st)
     aux[1].start()
@@ -240,19 +260,20 @@
     def spread(row):
         return jnp.transpose(jnp.broadcast_to(row, (cw, nf)))
 
+    loads[3].wait()
     for f in range(ls):
         wb[f + 1] = spread(w[pl.ds(f, 1), :])
-
     loads[4].wait()
 
-    def precondition(inst, before, order, p_message, q_message):
-        coupled = {}
-        for st in sts:
-            apply(st, "n", res, order, functools.partial(before, st), p_message, q_message)
-            coupled[st] = inner(st, res, part, every)
-        return coupled
-
-    def assemble(inst, st, target, coupled, p_message, q_message):
+    def second_half(st, s):
+        if st == 0 and s == ls - 2:
+            loads[5].wait()
+
+    def neumann_late(st, m):
+        late_face(st, "n", res, 0, m)
+        return inner(st, res, part, every)
+
+    def schur_early(inst, st, target, p_message, q_message):
         cs = columns(st)
         x32 = coarse_finish(inst, st)
         if inst == 0:
@@ -260,67 +281,75 @@
         else:
             x32 = x0[st] - alpha0[st] * x32
         x = x32.astype(BF16)
-        norm = coupled + column_sum(c32[st] * x[ncf:, :].astype(F32))
+        norm = column_sum(c32[st] * x[ncf:, :].astype(F32))
         for f in every:
             value = part[face(f), cs] + dot_first(con[pl.ds(f * ncf, ncf), :], x[f * ncf : (f + 1) * ncf, :])
             if f == 0:
                 value = value + receive(st, p_message)
-            if f == ls:
-                value = value + receive(st, q_message)
             target[face(f), cs] = value
+        early(st, "s", target, ls, q_message)
         return norm
 
-    def first_face(st, s):
-        if s != 0:
-            return
-        if st == 0:
-            aux[0].wait_recv()
-            wb[0] = spread(w_left[pl.ds(ls - 1, 1), :])
+    def schur_late(st, target, q_arrived, p_message):
+        cs = columns(st)
+        target[face(ls), cs] = target[face(ls), cs] + receive(st, q_arrived)
+        late_face(st, "s", target, ls, p_message)
+
+    x0, alpha0, norm0, bent0, coupled, norm = {}, {}, {}, {}, {}, {}
+
+    for st in sts:
+        early(st, "n", res, 0, N0_P, functools.partial(second_half, st))
+    aux[0].wait_recv()
+    wb[0] = spread(w_left[pl.ds(ls - 1, 1), :])
+    for st in sts:
         res[face(0), columns(st)] = receive(st, INIT_P)
-
-    nothing = lambda s: None
-
-    coupled = precondition(0, first_face, downward, N0_P, N0_Q)
+        coupled[st] = neumann_late(st, N0_Q)
     coarse_relay(0, 0)
-    loads[3].wait()
+    loads[6].wait()
     aux[1].wait_recv()
     aux[2].wait_recv()
-    loads[5].wait()
-    rows0 = {}
-    for st in sts:
-        norm = assemble(0, st, dirn, coupled[st], N0_P, N0_Q)
+    loads[7].wait()
+    for st in sts:
+        norm[st] = coupled[st] + schur_early(0, st, dirn, N0_P, S0_Q)
         if st + 1 < streams:
             coarse_relay(0, st + 1)
-        apply(st, "s", dirn, upward, nothing, S0_P, S0_Q)
-        reduce_start(slots1, 0, st, [norm, inner(st, dirn, part, every)])
-        coarse_start(1, st, restrict(st, part, every))
+    for st in sts:
+        schur_late(st, dirn, N0_Q, S0_P)
+        reduce_start(slots1, 0, st, [norm[st], inner(st, dirn, part, every)])
+    for st in sts:
+        cs = columns(st)
+        for f in owned:
+            value = part[face(f), cs]
+            if f == ls:
+                value = value + receive(st, S0_Q)
+            image[face(f), cs] = value
+        coarse_start(1, st, restrict(st, image, owned))
         coarse_send(1, st)
-    norm0, bent0, coupled = {}, {}, {}
-    for st in sts:
-        cs = columns(st)
+    for st in sts:
+        cs = columns(st)
+        kept = part[face(0), cs]
         total = reduce_finish(slots1, 0, st)
         norm0[st], bent0[st] = total[0:1], total[1:2]
         alpha0[st] = norm0[st] / bent0[st]
-        for f in every:
-            value = part[face(f), cs]
-            if f == 0:
-                value = value + receive(st, S0_P)
-            if f == ls:
-                value = value + receive(st, S0_Q)
-            image[face(f), cs] = value
-            res[face(f), cs] = res[face(f), cs] - alpha0[st] * value
-        apply(st, "n", res, downward, nothing, N1_P, N1_Q)
+        for f in owned:
+            res[face(f), cs] = res[face(f), cs] - alpha0[st] * image[face(f), cs]
+        early(st, "n", res, 0, N1_P)
+        res[face(0), cs] = res[face(0), cs] - alpha0[st] * (kept + receive(st, S0_P))
+        coupled[st] = neumann_late(st, N1_Q)
         c32[st] = restrict(st, res, owned)
-        coupled[st] = inner(st, res, part, every)
     coarse_relay(1, 0)
     for st in sts:
-        norm = assemble(1, st, zed, coupled[st], N1_P, N1_Q)
+        norm[st] = coupled[st] + schur_early(1, st, zed, N1_P, S1_Q)
         if st + 1 < streams:
             coarse_relay(1, st + 1)
-        apply(st, "s", zed, upward, nothing, None, S1_Q)
+    for st in sts:
+        schur_late(st, zed, N1_Q, None)
         reduce_start(slots2, 1, st, [
-            norm, inner(st, zed, part, every), inner(st, zed, image, owned), jnp.zeros_like(norm),
+            norm[st], inner(st, zed, part, every), inner(st, zed, image, owned), jnp.zeros_like(norm[st]),
         ])
+    for st in sts:
+        cs = columns(st)
+        part[face(ls), cs] = part[face(ls), cs] + receive(st, S1_Q)
     for st in sts:
         cs = columns(st)
         total = reduce_finish(slots2, 1, st)
@@ -332,10 +361,7 @@
             own = pl.ds((f - 1) * nf, nf)
             direction = zed[face(f), cs] + beta * dirn[face(f), cs]
             sol_ref[own, cs] = alpha0[st] * dirn[face(f), cs] + alpha1 * direction
-            value = part[face(f), cs]
-            if f == ls:
-                value = value + receive(st, S1_Q)
-            value = value + beta * image[face(f), cs]
+            value = part[face(f), cs] + beta * image[face(f), cs]
             out_ref[own, cs] = res[face(f), cs] - alpha1 * value
 
     for copy in aux:
@@ -381,7 +407,6 @@
             in_specs=[any_spec] * 6,
             out_specs=(vmem_spec,) * 2,
             scratch_shapes=[
-                pltpu.VMEM((rows, r), F32),
                 pltpu.VMEM((ls, nf), F32),
                 pltpu.VMEM((ls, nf), F32),
                 pltpu.VMEM(schur.shape, BF16),
@@ -397,10 +422,10 @@
                 pltpu.VMEM((streams, MESSAGES, nf, cw), BF16),
                 pltpu.VMEM((streams, MESSAGES, nf, cw), BF16),
                 pltpu.VMEM((streams, n // 2, 2, lc, cw), BF16),
-                pltpu.VMEM((streams, n // 2, 2, lc + ncf, cw), BF16),
+                pltpu.VMEM((streams, n // 2, 2, lc, cw), BF16),
                 pltpu.VMEM((streams, n, 2, cw), F32),
                 pltpu.VMEM((streams, n, 4, cw), F32),
-                pltpu.SemaphoreType.DMA((6,)),
+                pltpu.SemaphoreType.DMA((8,)),
                 pltpu.SemaphoreType.DMA((3, 2)),
                 pltpu.SemaphoreType.DMA((streams, MESSAGES)),
                 pltpu.SemaphoreType.DMA((streams, MESSAGES)),

time: 49.4 us -> 50.3 us (1.018)
  Pallas kernels: 48.6 us -> 49.3 us
    pallas_call x1, Pallas kernels: 47.3 us -> 48 us  [shards(): pl.pallas_call(functools.partial(kernel, n, streams), name='interface_cg'...]
where the time goes in v1:
time: 50.3 us; the launch traced here: 50.1 us
  Pallas kernels  49.3 us (98%)
  between operations  0.8 us (2%)
    pallas_call x1, Pallas kernels, shards(): pl.pallas_call(functools.partial(kernel, n, streams), name='interface_cg'...  48 us
    pallas_call x1, Pallas kernels, shards(): pl.pallas_call(deliver, name='deliver', out_shape=(jax.ShapeDtypeStruct((...  1.33 us

profile of v1, /device:TPU:0, one launch (start us, length us, event | category | flops | bytes accessed | tf_op | source)
XLA Modules:
  0.0 50.1 jit_solution(8551455285723064984)
XLA Ops:
  0.6 48.0 %interface_cg.1 = (f32[1024,256]{1,0:T(8,128)S(1)}, f32[1024,256]{1,0:T(8,128)S(1)}) custom-call(f32[1024,256]{1,0:T(8,128)} %rs_hbm.1, f32[2,512]{1,0:T(2,128)} %w_hbm.1, bf16[2048,1024]{1,0:T(8,128)(2,1)} %schur_hbm.1, bf16[2048,1024]{1,0:T(8,128)(2,1)} %neumann_hbm.1, bf16[64,512]{1,0:T(8,128)(2,1)} %con_hbm.1, bf16[64,1024]{1,0:T(8,128)(2,1)} %ainv_hbm.1), custom_call_target="tpu_custom_call" | custom-call | tf_op jit(solution)/shard_map/interface_cg/pallas_call | solution.py:403
  48.6 1.3 %deliver.1 = (f32[1024,256]{1,0:T(8,128)}, f32[1024,256]{1,0:T(8,128)}) custom-call(f32[1024,256]{1,0:T(8,128)S(1)} %get-tuple-element.4.sol_ref, f32[1024,256]{1,0:T(8,128)S(1)} %get-tuple-element.5.res_ref), custom_call_target="tpu_custom_call" | custom-call | tf_op jit(solution)/shard_map/deliver/pallas_call | solution.py:439

commit v2 on v1

--- a/solution.py
+++ b/solution.py
@@ -249,11 +249,11 @@
             (con_hbm.at[last_rows], con.at[pl.ds(0, ncf)]),
         ))
     ]
-    for st in sts:
+    aux[0].start()
+    message(0, INIT_P).start()
+    coarse_send(0, 0)
+    for st in sts[1:]:
         message(st, INIT_P).start()
-    aux[0].start()
-    for st in sts:
-        coarse_send(0, st)
     aux[1].start()
     aux[2].start()
 
@@ -299,9 +299,11 @@
 
     for st in sts:
         early(st, "n", res, 0, N0_P, functools.partial(second_half, st))
-    aux[0].wait_recv()
-    wb[0] = spread(w_left[pl.ds(ls - 1, 1), :])
-    for st in sts:
+        if st == 0:
+            for each in sts[1:]:
+                coarse_send(0, each)
+            aux[0].wait_recv()
+            wb[0] = spread(w_left[pl.ds(ls - 1, 1), :])
         res[face(0), columns(st)] = receive(st, INIT_P)
         coupled[st] = neumann_late(st, N0_Q)
     coarse_relay(0, 0)
@@ -313,7 +315,6 @@
         norm[st] = coupled[st] + schur_early(0, st, dirn, N0_P, S0_Q)
         if st + 1 < streams:
             coarse_relay(0, st + 1)
-    for st in sts:
         schur_late(st, dirn, N0_Q, S0_P)
         reduce_start(slots1, 0, st, [norm[st], inner(st, dirn, part, every)])
     for st in sts:
@@ -325,8 +326,6 @@
             image[face(f), cs] = value
         coarse_start(1, st, restrict(st, image, owned))
         coarse_send(1, st)
-    for st in sts:
-        cs = columns(st)
         kept = part[face(0), cs]
         total = reduce_finish(slots1, 0, st)
         norm0[st], bent0[st] = total[0:1], total[1:2]
@@ -342,7 +341,6 @@
         norm[st] = coupled[st] + schur_early(1, st, zed, N1_P, S1_Q)
         if st + 1 < streams:
             coarse_relay(1, st + 1)
-    for st in sts:
         schur_late(st, zed, N1_Q, None)
         reduce_start(slots2, 1, st, [
             norm[st], inner(st, zed, part, every), inner(st, zed, image, owned), jnp.zeros_like(norm[st]),

time: 50.3 us -> 46.3 us (0.920)
  Pallas kernels: 49.3 us -> 45.5 us
    pallas_call x1, Pallas kernels: 48 us -> 44.2 us  [shards(): pl.pallas_call(functools.partial(kernel, n, streams), name='interface_cg'...]
where the time goes in v2:
time: 46.3 us; the launch traced here: 46.2 us
  Pallas kernels  45.5 us (98%)
  between operations  0.64 us (1%)
    pallas_call x1, Pallas kernels, shards(): pl.pallas_call(functools.partial(kernel, n, streams), name='interface_cg'...  44.2 us
    pallas_call x1, Pallas kernels, shards(): pl.pallas_call(deliver, name='deliver', out_shape=(jax.ShapeDtypeStruct((...  1.33 us

profile of v2, /device:TPU:0, one launch (start us, length us, event | category | flops | bytes accessed | tf_op | source)
XLA Modules:
  0.0 46.2 jit_solution(11966883123768700950)
XLA Ops:
  0.6 44.2 %interface_cg.1 = (f32[1024,256]{1,0:T(8,128)S(1)}, f32[1024,256]{1,0:T(8,128)S(1)}) custom-call(f32[1024,256]{1,0:T(8,128)} %rs_hbm.1, f32[2,512]{1,0:T(2,128)} %w_hbm.1, bf16[2048,1024]{1,0:T(8,128)(2,1)} %schur_hbm.1, bf16[2048,1024]{1,0:T(8,128)(2,1)} %neumann_hbm.1, bf16[64,512]{1,0:T(8,128)(2,1)} %con_hbm.1, bf16[64,1024]{1,0:T(8,128)(2,1)} %ainv_hbm.1), custom_call_target="tpu_custom_call" | custom-call | tf_op jit(solution)/shard_map/interface_cg/pallas_call | solution.py:401
  44.8 1.3 %deliver.1 = (f32[1024,256]{1,0:T(8,128)}, f32[1024,256]{1,0:T(8,128)}) custom-call(f32[1024,256]{1,0:T(8,128)S(1)} %get-tuple-element.4.sol_ref, f32[1024,256]{1,0:T(8,128)S(1)} %get-tuple-element.5.res_ref), custom_call_target="tpu_custom_call" | custom-call | tf_op jit(solution)/shard_map/deliver/pallas_call | solution.py:437
